TPU v7x, 32 devices: a whole 2x2x4 slice. The times are simulated.
32 devices in a mesh: tile: 8 (over z, y), view: 4 (over x, core).
Axes of the slice: x: 2, y: 2, z: 4, core: 2. Of those that a mesh axis runs over, the one named last changes fastest.
Arguments:
- recorded: bfloat16 [4, 128, 256, 256], P('view', 'tile'), may hold values from 0.099609375 to 10
- estimate: float32 [128, 256, 256], P('tile', 'view'), may hold values from 0.5 to 2
- psf_taps: float32 [16, 3, 31], replicated, may hold values from 0.05 to 1
- half_width: int32 [16, 3], replicated, may hold values from 8 to 15
- assign: int32 [4], replicated, may hold values from 0 to 15
- flags: int32 [16, 32], P('tile', 'view'), may hold values 0 or 1
Outputs:
- restored: float32 [128, 256, 256], P('tile', 'view')
All inputs are finite; a program needn't handle non-finite values. No bound on the sum of `flags` on one device may be relied on, other than what follows from the above.
Results may differ from a plain program's by a relative error of at most 0.0007.
Values may be sent and summed in bfloat16 or wider, within the bound.
A program may use at most 64 MiB of HBM per device.

v0:
```python
import jax
import jax.numpy as jnp
from jax import lax
from jax.sharding import PartitionSpec as P

VIEWS = 4
KERNELS = 16
TAPS = 31


def padded_2(cells, sides, width):
    for axis, dim in sides:
        count = lax.axis_size(axis)
        ends = count - 1
        head = lax.slice_in_dim(cells, 0, width, axis=dim)
        tail = lax.slice_in_dim(cells, cells.shape[dim] - width, cells.shape[dim], axis=dim)
        cells = jnp.concatenate(
            [
                lax.ppermute(tail, axis, [(i, (i + 1) % count) for i in range(ends)]),
                cells,
                lax.ppermute(head, axis, [((i + 1) % count, i) for i in range(ends)]),
            ],
            axis=dim,
        )
    return cells


def make_kernels(psf_taps, half_width, assign):
    offsets = jnp.abs(jnp.arange(TAPS) - TAPS // 2)
    keep = (offsets[None, None, :] <= half_width[:, :, None]).astype(jnp.float32)
    raw = psf_taps * keep
    kern = raw / jnp.sum(raw, axis=-1, keepdims=True)
    picker = (assign[:, None] == jnp.arange(KERNELS)[None, :]).astype(jnp.float32)
    return jnp.einsum("sv,vaj->saj", picker, kern, precision=lax.Precision.HIGHEST)


def band_matrix(kernel, rows_count, cols_count, shift):
    rows = jnp.arange(rows_count)[:, None]
    cols = jnp.arange(cols_count)[None, :]
    offset = rows - cols + shift
    hits = (offset[None, :, :] == jnp.arange(TAPS)[:, None, None]).astype(jnp.float32)
    return jnp.sum(kernel[:, None, None] * hits, axis=0)


def along_second(volume, band):
    return jnp.einsum("xpz,pi->xiz", volume, band, precision=lax.Precision.HIGHEST)


def along_third(volume, band):
    return jnp.einsum("xyp,pi->xyi", volume, band, precision=lax.Precision.HIGHEST)


def shards(recorded, estimate, psf_taps, half_width, assign, flags):
    slab = estimate.shape[0]
    full_y = recorded.shape[2]
    depth_z = recorded.shape[3]
    kernels = make_kernels(psf_taps, half_width, assign)
    flipped = kernels[:, :, ::-1]
    slot = lax.axis_index("view")
    selector = (jnp.arange(VIEWS) == slot).astype(jnp.float32)
    own_kern = jnp.einsum("s,saj->aj", selector, kernels, precision=lax.Precision.HIGHEST)
    own_flip = jnp.einsum("s,saj->aj", selector, flipped, precision=lax.Precision.HIGHEST)
    padded_rows = slab + TAPS - 1
    first_own_flip = band_matrix(own_flip[0], padded_rows, slab, 0)
    second_own = band_matrix(own_kern[1], full_y, full_y, TAPS // 2)
    third_own = band_matrix(own_kern[2], depth_z, depth_z, TAPS // 2)
    second_flip = band_matrix(own_flip[1], full_y, full_y, TAPS // 2)
    third_flip = band_matrix(own_flip[2], depth_z, depth_z, TAPS // 2)
    first_all = jnp.stack([band_matrix(kernels[s, 0], padded_rows, slab, 0) for s in range(VIEWS)])
    cells = jnp.repeat(jnp.repeat(flags, 8, axis=0), 8, axis=1)[:, :, None] > 0
    data_slab = recorded[0].astype(jnp.float32)
    current = estimate
    rounded = current.astype(jnp.bfloat16)
    padded = padded_2(rounded, (("tile", 0),), TAPS // 2).astype(jnp.float32)
    stacked = jnp.einsum("pyz,spi->siyz", padded, first_all, precision=lax.Precision.HIGHEST)
    first_pass = lax.all_to_all(
        stacked.astype(jnp.bfloat16), "view", split_axis=0, concat_axis=2, tiled=True
    ).astype(stacked.dtype)[0]
    blurred = along_third(along_second(first_pass, second_own), third_own)
    ratio = (data_slab / blurred).astype(jnp.bfloat16)
    padded_ratio = padded_2(ratio, (("tile", 0),), TAPS // 2).astype(jnp.float32)
    back = jnp.einsum("pyz,pi->iyz", padded_ratio, first_own_flip, precision=lax.Precision.HIGHEST)
    back = along_third(along_second(back, second_flip), third_flip)
    total = lax.psum_scatter(back, "view", scatter_dimension=1, tiled=True)
    correction = total / VIEWS
    current = jnp.where(cells, current * correction, current)
    return current


def solution(mesh):
    placed = (
        P("view", "tile", None, None),
        P("tile", "view", None),
        P(),
        P(),
        P(),
        P("tile", "view"),
    )
    return jax.shard_map(
        shards, mesh=mesh, in_specs=placed, out_specs=P("tile", "view", None), check_vma=False
    )
```

profile of v0, /device:TPU:0, one launch (start us, length us, event | category | flops | bytes accessed | tf_op | source)
XLA Modules:
  0.0 236.5 jit_solution(3409513282182263963)
XLA Ops:
  6.5 1.8 copy.35
  8.3 0.2 fusion.52
  8.6 4.9 %collective-permute-start = (bf16[15,64,256]{2,0,1:T(8,128)(2,1)S(1)}, bf16[15,64,256]{2,0,1:T(8,128)(2,1)S(1)}, u32[]{:S(2)}, u32[]{:S(2)}) collective-permute-start(bf16[15,64,256]{2,0,1:T(8,128)(2,1)S(1)} %get-tuple-element.16), channel_id=1, source_target_pairs={{0,4},{4,8},{8,12},{12,16},{16,20},{20,24},{24,28},{1,5},{5,9},{9,... | collective-permute-start | bytes 1474568 | tf_op jit(solution)/shard_map/ppermute | solution.py:19
  13.5 1.3 collective-permute-start.1
  14.8 0.9 fusion.29
  15.7 0.9 fusion.27
  16.7 0.1 rev.3
  16.8 0.1 fusion.37
  16.9 0.1 fusion.39
  17.1 0.2 select_reduce_fusion.8
  17.3 18.6 %collective-permute-done = bf16[15,64,256]{2,0,1:T(8,128)(2,1)S(1)} collective-permute-done((bf16[15,64,256]{2,0,1:T(8,128)(2,1)S(1)}, bf16[15,64,256]{2,0,1:T(8,128)(2,1)S(1)}, u32[]{:S(2)}, u32[]{:S(2)}) %collective-permute-start) | collective-permute-done | bytes 491552 | tf_op jit(solution)/shard_map/ppermute | solution.py:19
  35.9 3.2 %convolution_convert_fusion = bf16[4,16,64,256]{3,1,2,0:T(8,128)(2,1)} fusion(bf16[15,64,256]{2,0,1:T(8,128)(2,1)S(1)} %collective-permute-done.1, bf16[16,64,256]{2,0,1:T(8,128)(2,1)S(1)} %copy.35, bf16[15,64,256]{2,0,1:T(8,128)(2,1)S(1)} %collective-permute-done, f32[1,46,16]{1,2,0:T(8,128)S(1)} %bitcast.83, f32[1,46,16]{1,2,0:T(8,128)S(1)} %bitcast.84, ...), kind=kOutput, calls=%fused_computation.18 | convolution fusion | flops 584393344 | bytes 3616256 | tf_op jit(solution)/shard_map/pyz,spi->siyz/dot_general | solution.py:75
  39.0 3.6 %all-to-all-start = ((bf16[4,16,64,256]{3,1,2,0:T(8,128)(2,1)}), bf16[4,16,64,256]{3,1,2,0:T(8,128)(2,1)S(1)}, u32[]{:S(2)}, u32[]{:S(2)}) async-start(bf16[4,16,64,256]{3,1,2,0:T(8,128)(2,1)} %convolution_convert_fusion), calls=%async_computation | async-start | bytes 4194304 | tf_op jit(solution)/shard_map/all_to_all | solution.py:76
  42.6 0.0 reduce-scatter.2.cloned.1.call-start
  42.7 3.6 %select_reduce_fusion = (f32[256,256]{1,0:T(8,128)S(1)}, f32[256,256]{1,0:T(8,128)S(1)}, f32[256,256]{1,0:T(8,128)S(1)}, f32[256,256]{1,0:T(8,128)S(1)}) fusion(f32[31]{0:T(128)S(1)} %get-tuple-element.28, s32[256,256]{1,0:T(8,128)S(1)} %subtract_add_fusion, f32[31]{0:T(128)S(1)} %get-tuple-element.26, f32[31]{0:T(128)S(1)} %get-tuple-element.25, ...), kind=kLoop, calls=%fused_computation | loop fusion | flops 18022400 | bytes 1311216 | tf_op jit(solution)/shard_map/reduce_sum | solution.py:42
  46.4 21.9 %all-to-all-done = bf16[4,16,64,256]{3,1,2,0:T(8,128)(2,1)S(1)} async-done(((bf16[4,16,64,256]{3,1,2,0:T(8,128)(2,1)}), bf16[4,16,64,256]{3,1,2,0:T(8,128)(2,1)S(1)}, u32[]{:S(2)}, u32[]{:S(2)}) %all-to-all-start) | async-done | bytes 2097184 | tf_op jit(solution)/shard_map/all_to_all | solution.py:76
  68.3 2.2 fusion.9
  70.5 3.7 %fusion.2 = bf16[16,256,256]{2,1,0:T(8,128)(2,1)S(1)} fusion(bf16[1,16,256,256]{3,2,1,0:T(8,128)(2,1)S(1)} %copy-done.1, f32[256,16,256]{2,0,1:T(8,128)S(1)} %fusion.9, f32[256,256]{1,0:T(8,128)S(1)} %get-tuple-element.6), kind=kOutput, calls=%fused_computation.9 | convolution fusion | flops 3224371200 | bytes 8650752 | tf_op jit(solution)/shard_map/xyp,pi->xyi/dot_general | solution.py:50
  74.2 0.4 fusion.51
  74.6 4.5 %collective-permute-start.2 = (bf16[15,256,256]{2,1,0:T(8,128)(2,1)S(1)}, bf16[15,256,256]{2,1,0:T(8,128)(2,1)S(1)}, u32[]{:S(2)}, u32[]{:S(2)}) collective-permute-start(bf16[15,256,256]{2,1,0:T(8,128)(2,1)S(1)} %get-tuple-element.14), channel_id=1, source_target_pairs={{0,4},{4,8},{8,12},{12,16},{16,20},{20,24},{24,28},{1,5},{5,9},{9,... | collective-permute-start | bytes 5898248 | tf_op jit(solution)/shard_map/ppermute | solution.py:19
  79.1 1.5 collective-permute-start.3
  80.6 82.3 %collective-permute-done.2 = bf16[15,256,256]{2,1,0:T(8,128)(2,1)S(1)} collective-permute-done((bf16[15,256,256]{2,1,0:T(8,128)(2,1)S(1)}, bf16[15,256,256]{2,1,0:T(8,128)(2,1)S(1)}, u32[]{:S(2)}, u32[]{:S(2)}) %collective-permute-start.2) | collective-permute-done | bytes 1966112 | tf_op jit(solution)/shard_map/ppermute | solution.py:19
  162.9 0.9 pad_maximum_fusion
  163.8 5.3 %fusion = f32[16,256,256]{2,0,1:T(8,128)S(1)} fusion(bf16[46,256,256]{2,1,0:T(8,128)(2,1)S(1)} %pad_maximum_fusion, f32[46,16]{0,1:T(8,128)S(1)} %get-tuple-element.9), kind=kOutput, calls=%fused_computation.5 | convolution fusion | flops 578813952 | bytes 10226560 | tf_op jit(solution)/shard_map/pyz,pi->iyz/dot_general | solution.py:82
  169.1 6.3 %fusion.7 = f32[256,16,256]{2,0,1:T(8,128)S(1)} fusion(f32[16,256,256]{2,0,1:T(8,128)S(1)} %fusion, f32[256,256]{1,0:T(8,128)S(1)} %get-tuple-element.8), kind=kOutput, calls=%fused_computation.14 | convolution fusion | flops 3221225472 | bytes 8650752 | tf_op jit(solution)/shard_map/xpz,pi->xiz/dot_general | solution.py:46
  175.4 5.0 %fusion.3 = f32[16,256,256]{2,1,0:T(8,128)} fusion(f32[256,16,256]{2,0,1:T(8,128)S(1)} %fusion.7, f32[256,256]{1,0:T(8,128)S(1)} %get-tuple-element.5), kind=kOutput, calls=%fused_computation.10 | convolution fusion | flops 3221225472 | bytes 8650752 | tf_op jit(solution)/shard_map/xyp,pi->xyi/dot_general | solution.py:50
  180.3 0.0 reduce-scatter.2.cloned.1.call-update
  180.4 0.7 copy-done.2
  181.0 0.1 copy.11
  181.1 0.1 copy.12
  181.2 46.1 %reduce-scatter.2.cloned.1.call-done = f32[16,64,256]{2,1,0:T(8,128)} async-done(((f32[16,256,256]{2,1,0:T(8,128)}), f32[16,64,256]{2,1,0:T(8,128)}) %reduce-scatter.2.cloned.1.call-update) | async-done | bytes 1048592 | tf_op jit(solution)/shard_map/reduce_scatter | solution.py:84
  227.3 2.4 %multiply_select_fusion = f32[16,64,256]{2,1,0:T(8,128)} fusion(f32[16,64,256]{2,1,0:T(8,128)S(1)} %copy-done, f32[16,64,256]{2,1,0:T(8,128)} %reduce-scatter.2.cloned.1.call-done, pred[16,64]{1,0:T(8,128)(4,1)S(1)} %copy.12), kind=kLoop, calls=%fused_computation.24 | loop fusion | flops 786432 | bytes 3146752 | tf_op jit(solution)/shard_map/jit(_where)/select_n | solution.py:86
  (17 shorter events, 0.1 us)
Async XLA Ops:
  8.6 27.3 %collective-permute-start = (bf16[15,64,256]{2,0,1:T(8,128)(2,1)S(1)}, bf16[15,64,256]{2,0,1:T(8,128)(2,1)S(1)}, u32[]{:S(2)}, u32[]{:S(2)}) collective-permute-start(bf16[15,64,256]{2,0,1:T(8,128)(2,1)S(1)} %get-tuple-element.16), channel_id=1, source_target_pairs={{0,4},{4,8},{8,12},{12,16},{16,20},{20,24},{24,28},{1,5},{5,9},{9,... | collective-permute-start | bytes 1474568 | tf_op jit(solution)/shard_map/ppermute | solution.py:19
  13.5 22.4 %collective-permute-start.1 = (bf16[15,64,256]{2,0,1:T(8,128)(2,1)S(1)}, bf16[15,64,256]{2,0,1:T(8,128)(2,1)S(1)}, u32[]{:S(2)}, u32[]{:S(2)}) collective-permute-start(bf16[15,64,256]{2,0,1:T(8,128)(2,1)S(1)} %get-tuple-element.17), channel_id=1, source_target_pairs={{4,0},{8,4},{12,8},{16,12},{20,16},{24,20},{28,24},{5,1},{9,5},{13... | collective-permute-start | bytes 1474568 | tf_op jit(solution)/shard_map/ppermute | solution.py:21
  39.0 29.2 %all-to-all-start = ((bf16[4,16,64,256]{3,1,2,0:T(8,128)(2,1)}), bf16[4,16,64,256]{3,1,2,0:T(8,128)(2,1)S(1)}, u32[]{:S(2)}, u32[]{:S(2)}) async-start(bf16[4,16,64,256]{3,1,2,0:T(8,128)(2,1)} %convolution_convert_fusion), calls=%async_computation | async-start | bytes 4194304 | tf_op jit(solution)/shard_map/all_to_all | solution.py:76
  42.6 184.7 %reduce-scatter.2.cloned.1.call-start = ((), (), s32[]{:S(2)}) async-start(), calls=%async_computation.2 | async-start | bytes 5242880 | tf_op jit(solution)/shard_map/reduce_scatter | solution.py:84
  68.3 2.2 copy-start.1
  74.6 88.3 %collective-permute-start.2 = (bf16[15,256,256]{2,1,0:T(8,128)(2,1)S(1)}, bf16[15,256,256]{2,1,0:T(8,128)(2,1)S(1)}, u32[]{:S(2)}, u32[]{:S(2)}) collective-permute-start(bf16[15,256,256]{2,1,0:T(8,128)(2,1)S(1)} %get-tuple-element.14), channel_id=1, source_target_pairs={{0,4},{4,8},{8,12},{12,16},{16,20},{20,24},{24,28},{1,5},{5,9},{9,... | collective-permute-start | bytes 5898248 | tf_op jit(solution)/shard_map/ppermute | solution.py:19
  79.1 83.8 %collective-permute-start.3 = (bf16[15,256,256]{2,1,0:T(8,128)(2,1)S(1)}, bf16[15,256,256]{2,1,0:T(8,128)(2,1)S(1)}, u32[]{:S(2)}, u32[]{:S(2)}) collective-permute-start(bf16[15,256,256]{2,1,0:T(8,128)(2,1)S(1)} %get-tuple-element.15), channel_id=1, source_target_pairs={{4,0},{8,4},{12,8},{16,12},{20,16},{24,20},{28,24},{5,1},{9,5},{13... | collective-permute-start | bytes 5898248 | tf_op jit(solution)/shard_map/ppermute | solution.py:21
  180.3 0.7 copy-start.2
  180.3 47.0 %copy-start = (f32[16,64,256]{2,1,0:T(8,128)S(1)}, f32[16,64,256]{2,1,0:T(8,128)}, u32[]{:S(2)}) copy-start(f32[16,64,256]{2,1,0:T(8,128)} %param.7) | copy-start | bytes 3145732
Sparse Core Ops, SparseCore 0:
  180.5 46.7 reduce-scatter.1
where the time goes:
time: 237 us
  waiting for transfers between devices  169 us (71%)
  matrix products  26.7 us (11%)
  starting transfers between devices  15.9 us (7%)
  between operations  13.6 us (6%)
  other arithmetic  8.14 us (3%)
  local copies, waits for them, and re-layouts  3.41 us (1%)
    ppermute x2, waiting for transfers between devices, padded_2(): lax.ppermute(tail, axis, [(i, (i + 1) % count) for i in range(ends)])  101 us
    reduce_scatter x1, waiting for transfers between devices, shards(): total = lax.psum_scatter(back, 'view', scatter_dimension=1, tiled=True)  46.1 us
    all_to_all x1, waiting for transfers between devices, shards(): lax.all_to_all(stacked.astype(jnp.bfloat16), 'view', split_axis=0, concat...  21.9 us
    ppermute x2, starting transfers between devices, padded_2(): lax.ppermute(tail, axis, [(i, (i + 1) % count) for i in range(ends)])  9.45 us
    dot_general x2, matrix products, along_third(): jnp.einsum('xyp,pi->xyi', volume, band, precision=lax.Precision.HIGHEST)  8.62 us
    dot_general x2, matrix products, along_second(): jnp.einsum('xpz,pi->xiz', volume, band, precision=lax.Precision.HIGHEST)  8.45 us
    dot_general x1, matrix products, shards(): jnp.einsum('pyz,pi->iyz', padded_ratio, first_own_flip, precision=lax.Pre...  5.27 us
  transfers between devices with their start and end apart: 6, of which 4 were waited for; matrix products, arithmetic and copies ran while one was open for 3% of the time, Pallas kernels for 0%

commit v1 on v0

--- a/solution.py
+++ b/solution.py
@@ -6,6 +6,29 @@
 VIEWS = 4
 KERNELS = 16
 TAPS = 31
+
+
+def in_blocks(x, dim, size):
+    shape = x.shape
+    pieces = x.reshape(*shape[:dim], size, shape[dim] // size, *shape[dim + 1 :])
+    return jnp.moveaxis(pieces, dim, 0)
+
+
+def joined_along(pieces, dim):
+    shape = list(pieces.shape[1:])
+    shape[dim] *= pieces.shape[0]
+    return jnp.moveaxis(pieces, 0, dim).reshape(shape)
+
+
+def exchange_directly(x, axis, split_dim, concat_dim):
+    size, index = (lax.axis_size(axis), lax.axis_index(axis))
+    blocks = in_blocks(x, split_dim, size)
+    gathered = [blocks[index]]
+    for step in range(1, size):
+        sent = blocks[(index + step) % size]
+        gathered.append(lax.ppermute(sent, axis, [(i, (i + step) % size) for i in range(size)]))
+    blocks = jnp.stack(gathered)[(index - jnp.arange(size)) % size]
+    return joined_along(blocks, concat_dim)
 
 
 def padded_2(cells, sides, width):
@@ -73,9 +96,9 @@
     rounded = current.astype(jnp.bfloat16)
     padded = padded_2(rounded, (("tile", 0),), TAPS // 2).astype(jnp.float32)
     stacked = jnp.einsum("pyz,spi->siyz", padded, first_all, precision=lax.Precision.HIGHEST)
-    first_pass = lax.all_to_all(
-        stacked.astype(jnp.bfloat16), "view", split_axis=0, concat_axis=2, tiled=True
-    ).astype(stacked.dtype)[0]
+    first_pass = exchange_directly(stacked.astype(jnp.bfloat16), "view", 0, 2).astype(
+        stacked.dtype
+    )[0]
     blurred = along_third(along_second(first_pass, second_own), third_own)
     ratio = (data_slab / blurred).astype(jnp.bfloat16)
     padded_ratio = padded_2(ratio, (("tile", 0),), TAPS // 2).astype(jnp.float32)

time: 237 us -> 236 us (level)
  local copies, waits for them, and re-layouts: 3.41 us -> 5.88 us
    all_to_all x1 -> x0, waiting for transfers between devices: 21.9 us -> none  [shards(): lax.all_to_all(stacked.astype(jnp.bfloat16), 'view', split_axis=0, concat...]
    ppermute x0 -> x3, waiting for transfers between devices: none -> 17.9 us  [exchange_directly(): lax.ppermute(sent, axis, [(i, (i + step) % size) for i in range(size)])]
    all_to_all x1 -> x0, starting transfers between devices: 3.61 us -> none  [shards(): lax.all_to_all(stacked.astype(jnp.bfloat16), 'view', split_axis=0, concat...]
    ppermute x0 -> x3, starting transfers between devices: none -> 3 us  [exchange_directly(): lax.ppermute(sent, axis, [(i, (i + step) % size) for i in range(size)])]
    ppermute x2, waiting for transfers between devices: 101 us -> 103 us  [padded_2(): lax.ppermute(tail, axis, [(i, (i + 1) % count) for i in range(ends)])]
  transfers between devices with their start and end apart: 6 -> 8, of which waited for: 4 -> 6; matrix products, arithmetic and copies ran while one was open for 3% -> 2% of each run, Pallas kernels for 0% -> 0%
where the time goes in v1:
time: 236 us
  waiting for transfers between devices  167 us (71%)
  matrix products  24.6 us (10%)
  starting transfers between devices  15.2 us (6%)
  between operations  13.7 us (6%)
  other arithmetic  9.02 us (4%)
  local copies, waits for them, and re-layouts  5.88 us (2%)
    ppermute x2, waiting for transfers between devices, padded_2(): lax.ppermute(tail, axis, [(i, (i + 1) % count) for i in range(ends)])  103 us
    reduce_scatter x1, waiting for transfers between devices, shards(): total = lax.psum_scatter(back, 'view', scatter_dimension=1, tiled=True)  46 us
    ppermute x3, waiting for transfers between devices, exchange_directly(): lax.ppermute(sent, axis, [(i, (i + step) % size) for i in range(size)])  17.9 us
    ppermute x2, starting transfers between devices, padded_2(): lax.ppermute(tail, axis, [(i, (i + 1) % count) for i in range(ends)])  9.44 us
    dot_general x2, matrix products, along_third(): jnp.einsum('xyp,pi->xyi', volume, band, precision=lax.Precision.HIGHEST)  8.61 us
    dot_general x2, matrix products, along_second(): jnp.einsum('xpz,pi->xiz', volume, band, precision=lax.Precision.HIGHEST)  8.45 us
    dot_general x1, matrix products, shards(): jnp.einsum('pyz,pi->iyz', padded_ratio, first_own_flip, precision=lax.Pre...  5.27 us
  transfers between devices with their start and end apart: 8, of which 6 were waited for; matrix products, arithmetic and copies ran while one was open for 2% of the time, Pallas kernels for 0%

profile of v1, /device:TPU:0, one launch (start us, length us, event | category | flops | bytes accessed | tf_op | source)
XLA Modules:
  0.0 235.7 jit_solution(6731506186799451247)
XLA Ops:
  6.5 1.8 copy.35
  8.4 0.2 fusion.54
  8.6 4.9 %collective-permute-start = (bf16[15,64,256]{2,0,1:T(8,128)(2,1)S(1)}, bf16[15,64,256]{2,0,1:T(8,128)(2,1)S(1)}, u32[]{:S(2)}, u32[]{:S(2)}) collective-permute-start(bf16[15,64,256]{2,0,1:T(8,128)(2,1)S(1)} %get-tuple-element.20), channel_id=1, source_target_pairs={{0,4},{4,8},{8,12},{12,16},{16,20},{20,24},{24,28},{1,5},{5,9},{9,... | collective-permute-start | bytes 1474568 | tf_op jit(solution)/shard_map/ppermute | solution.py:42
  13.5 1.3 collective-permute-start.1
  14.9 0.2 fusion.29
  15.0 0.2 fusion.27
  15.5 0.1 fusion.39
  15.8 0.2 select_reduce_fusion.8
  16.0 19.9 %collective-permute-done = bf16[15,64,256]{2,0,1:T(8,128)(2,1)S(1)} collective-permute-done((bf16[15,64,256]{2,0,1:T(8,128)(2,1)S(1)}, bf16[15,64,256]{2,0,1:T(8,128)(2,1)S(1)}, u32[]{:S(2)}, u32[]{:S(2)}) %collective-permute-start) | collective-permute-done | bytes 491552 | tf_op jit(solution)/shard_map/ppermute | solution.py:42
  35.9 1.8 convolution_convert_fusion
  37.7 0.1 dynamic-slice_bitcast_fusion
  37.9 1.6 collective-permute-start.3
  39.5 1.4 collective-permute-start.4
  40.9 3.6 %select_reduce_fusion = (f32[256,256]{1,0:T(8,128)S(1)}, f32[256,256]{1,0:T(8,128)S(1)}, f32[256,256]{1,0:T(8,128)S(1)}, f32[256,256]{1,0:T(8,128)S(1)}) fusion(f32[31]{0:T(128)S(1)} %get-tuple-element.32, s32[256,256]{1,0:T(8,128)S(1)} %subtract_add_fusion, f32[31]{0:T(128)S(1)} %get-tuple-element.30, f32[31]{0:T(128)S(1)} %get-tuple-element.29, ...), kind=kLoop, calls=%fused_computation.1 | loop fusion | flops 18022400 | bytes 1311216 | tf_op jit(solution)/shard_map/reduce_sum | solution.py:65
  44.5 7.0 %collective-permute-done.2 = bf16[1,16,64,256]{3,1,2,0:T(8,128)(2,1)S(1)} collective-permute-done((bf16[1,16,64,256]{3,1,2,0:T(8,128)(2,1)S(1)}, bf16[1,16,64,256]{3,1,2,0:T(8,128)(2,1)S(1)}, u32[]{:S(2)}, u32[]{:S(2)}) %collective-permute-start.2) | collective-permute-done | bytes 524320 | tf_op jit(solution)/shard_map/ppermute | solution.py:29
  51.5 1.3 collective-permute-done.3
  52.8 9.6 %collective-permute-done.4 = bf16[1,16,64,256]{3,1,2,0:T(8,128)(2,1)S(1)} collective-permute-done((bf16[1,16,64,256]{3,1,2,0:T(8,128)(2,1)S(1)}, bf16[1,16,64,256]{3,1,2,0:T(8,128)(2,1)S(1)}, u32[]{:S(2)}, u32[]{:S(2)}) %collective-permute-start.4) | collective-permute-done | bytes 524320 | tf_op jit(solution)/shard_map/ppermute | solution.py:29
  62.4 1.6 maximum_bitcast_fusion
  64.0 2.3 gather_fusion
  66.3 2.2 fusion.9
  68.5 3.7 %fusion.2 = bf16[16,256,256]{2,1,0:T(8,128)(2,1)S(1)} fusion(bf16[1,16,256,256]{3,2,1,0:T(8,128)(2,1)S(1)} %copy-done.3, f32[256,16,256]{2,0,1:T(8,128)S(1)} %fusion.9, f32[256,256]{1,0:T(8,128)S(1)} %get-tuple-element.6), kind=kOutput, calls=%fused_computation.10 | convolution fusion | flops 3224371200 | bytes 8650752 | tf_op jit(solution)/shard_map/xyp,pi->xyi/dot_general | solution.py:73
  72.2 0.4 fusion.53
  72.6 4.5 %collective-permute-start.5 = (bf16[15,256,256]{2,1,0:T(8,128)(2,1)S(1)}, bf16[15,256,256]{2,1,0:T(8,128)(2,1)S(1)}, u32[]{:S(2)}, u32[]{:S(2)}) collective-permute-start(bf16[15,256,256]{2,1,0:T(8,128)(2,1)S(1)} %get-tuple-element.14), channel_id=1, source_target_pairs={{0,4},{4,8},{8,12},{12,16},{16,20},{20,24},{24,28},{1,5},{5,9},{9,... | collective-permute-start | bytes 5898248 | tf_op jit(solution)/shard_map/ppermute | solution.py:42
  77.1 1.5 collective-permute-start.6
  78.6 83.6 %collective-permute-done.5 = bf16[15,256,256]{2,1,0:T(8,128)(2,1)S(1)} collective-permute-done((bf16[15,256,256]{2,1,0:T(8,128)(2,1)S(1)}, bf16[15,256,256]{2,1,0:T(8,128)(2,1)S(1)}, u32[]{:S(2)}, u32[]{:S(2)}) %collective-permute-start.5) | collective-permute-done | bytes 1966112 | tf_op jit(solution)/shard_map/ppermute | solution.py:42
  162.2 0.9 pad_maximum_fusion
  163.1 5.3 %fusion = f32[16,256,256]{2,0,1:T(8,128)S(1)} fusion(bf16[46,256,256]{2,1,0:T(8,128)(2,1)S(1)} %pad_maximum_fusion, f32[46,16]{0,1:T(8,128)S(1)} %get-tuple-element.9), kind=kOutput, calls=%fused_computation.6 | convolution fusion | flops 578813952 | bytes 10226560 | tf_op jit(solution)/shard_map/pyz,pi->iyz/dot_general | solution.py:105
  168.4 6.3 %fusion.7 = f32[256,16,256]{2,0,1:T(8,128)S(1)} fusion(f32[16,256,256]{2,0,1:T(8,128)S(1)} %fusion, f32[256,256]{1,0:T(8,128)S(1)} %get-tuple-element.8), kind=kOutput, calls=%fused_computation.15 | convolution fusion | flops 3221225472 | bytes 8650752 | tf_op jit(solution)/shard_map/xpz,pi->xiz/dot_general | solution.py:69
  174.7 5.0 %fusion.3 = f32[16,256,256]{2,1,0:T(8,128)} fusion(f32[256,16,256]{2,0,1:T(8,128)S(1)} %fusion.7, f32[256,256]{1,0:T(8,128)S(1)} %get-tuple-element.5), kind=kOutput, calls=%fused_computation.11 | convolution fusion | flops 3221225472 | bytes 8650752 | tf_op jit(solution)/shard_map/xyp,pi->xyi/dot_general | solution.py:73
  179.6 0.7 copy-done.4
  180.5 46.0 %reduce-scatter.2.cloned.1.call-done = f32[16,64,256]{2,1,0:T(8,128)} async-done(((f32[16,256,256]{2,1,0:T(8,128)}), f32[16,64,256]{2,1,0:T(8,128)}) %reduce-scatter.2.cloned.1.call-update) | async-done | bytes 1048592 | tf_op jit(solution)/shard_map/reduce_scatter | solution.py:107
  226.4 2.4 %multiply_select_fusion = f32[16,64,256]{2,1,0:T(8,128)} fusion(f32[16,64,256]{2,1,0:T(8,128)S(1)} %copy-done, f32[16,64,256]{2,1,0:T(8,128)} %reduce-scatter.2.cloned.1.call-done, pred[16,64]{1,0:T(8,128)(4,1)S(1)} %copy.12), kind=kLoop, calls=%fused_computation.26 | loop fusion | flops 786432 | bytes 3146752 | tf_op jit(solution)/shard_map/jit(_where)/select_n | solution.py:109
  (32 shorter events, 0.6 us)
Async XLA Ops:
  6.5 8.3 %copy-start.1 = (f32[16,3,31]{2,0,1:T(8,128)S(1)}, f32[16,3,31]{2,0,1:T(8,128)}, u32[]{:S(2)}) copy-start(f32[16,3,31]{2,0,1:T(8,128)} %param.8) | copy-start | bytes 17860
  6.5 8.3 %copy-start.2 = (s32[16,3]{0,1:T(4,128)S(1)}, s32[16,3]{0,1:T(4,128)}, u32[]{:S(2)}) copy-start(s32[16,3]{0,1:T(4,128)} %param.9) | copy-start | bytes 580
  6.5 8.5 %copy-start.5 = (s32[4]{0:T(128)S(1)}, s32[4]{0:T(128)}, u32[]{:S(2)}) copy-start(s32[4]{0:T(128)} %param.10) | copy-start | bytes 52
  6.5 219.9 %reduce-scatter.2.cloned.1.call-start = ((), (), s32[]{:S(2)}) async-start(), calls=%async_computation.1 | async-start | bytes 5242880 | tf_op jit(solution)/shard_map/reduce_scatter | solution.py:107
  8.6 27.3 %collective-permute-start = (bf16[15,64,256]{2,0,1:T(8,128)(2,1)S(1)}, bf16[15,64,256]{2,0,1:T(8,128)(2,1)S(1)}, u32[]{:S(2)}, u32[]{:S(2)}) collective-permute-start(bf16[15,64,256]{2,0,1:T(8,128)(2,1)S(1)} %get-tuple-element.20), channel_id=1, source_target_pairs={{0,4},{4,8},{8,12},{12,16},{16,20},{20,24},{24,28},{1,5},{5,9},{9,... | collective-permute-start | bytes 1474568 | tf_op jit(solution)/shard_map/ppermute | solution.py:42
  13.5 22.4 %collective-permute-start.1 = (bf16[15,64,256]{2,0,1:T(8,128)(2,1)S(1)}, bf16[15,64,256]{2,0,1:T(8,128)(2,1)S(1)}, u32[]{:S(2)}, u32[]{:S(2)}) collective-permute-start(bf16[15,64,256]{2,0,1:T(8,128)(2,1)S(1)} %get-tuple-element.21), channel_id=1, source_target_pairs={{4,0},{8,4},{12,8},{16,12},{20,16},{24,20},{28,24},{5,1},{9,5},{13... | collective-permute-start | bytes 1474568 | tf_op jit(solution)/shard_map/ppermute | solution.py:44
  37.9 13.6 %collective-permute-start.2 = (bf16[1,16,64,256]{3,1,2,0:T(8,128)(2,1)S(1)}, bf16[1,16,64,256]{3,1,2,0:T(8,128)(2,1)S(1)}, u32[]{:S(2)}, u32[]{:S(2)}) collective-permute-start(bf16[1,16,64,256]{3,1,2,0:T(8,128)(2,1)S(1)} %get-tuple-element.19), channel_id=1, source_target_pairs={{0,1},{1,2},{2,3},{3,0},{4,5},{5,6},{6,7},{7,4},{8,9},{9,10},{10,1... | collective-permute-start | bytes 1572872 | tf_op jit(solution)/shard_map/ppermute | solution.py:29
  37.9 14.9 %collective-permute-start.3 = (bf16[1,16,64,256]{3,1,2,0:T(8,128)(2,1)S(1)}, bf16[1,16,64,256]{3,1,2,0:T(8,128)(2,1)S(1)}, u32[]{:S(2)}, u32[]{:S(2)}) collective-permute-start(bf16[1,16,64,256]{3,1,2,0:T(8,128)(2,1)S(1)} %get-tuple-element.18), channel_id=1, source_target_pairs={{0,2},{1,3},{2,0},{3,1},{4,6},{5,7},{6,4},{7,5},{8,10},{9,11},{10,... | collective-permute-start | bytes 1572872 | tf_op jit(solution)/shard_map/ppermute | solution.py:29
  39.5 22.9 %collective-permute-start.4 = (bf16[1,16,64,256]{3,1,2,0:T(8,128)(2,1)S(1)}, bf16[1,16,64,256]{3,1,2,0:T(8,128)(2,1)S(1)}, u32[]{:S(2)}, u32[]{:S(2)}) collective-permute-start(bf16[1,16,64,256]{3,1,2,0:T(8,128)(2,1)S(1)} %get-tuple-element.17), channel_id=1, source_target_pairs={{0,3},{1,0},{2,1},{3,2},{4,7},{5,4},{6,5},{7,6},{8,11},{9,8},{10,9... | collective-permute-start | bytes 1572872 | tf_op jit(solution)/shard_map/ppermute | solution.py:29
  66.3 2.2 copy-start.3
  72.6 89.6 %collective-permute-start.5 = (bf16[15,256,256]{2,1,0:T(8,128)(2,1)S(1)}, bf16[15,256,256]{2,1,0:T(8,128)(2,1)S(1)}, u32[]{:S(2)}, u32[]{:S(2)}) collective-permute-start(bf16[15,256,256]{2,1,0:T(8,128)(2,1)S(1)} %get-tuple-element.14), channel_id=1, source_target_pairs={{0,4},{4,8},{8,12},{12,16},{16,20},{20,24},{24,28},{1,5},{5,9},{9,... | collective-permute-start | bytes 5898248 | tf_op jit(solution)/shard_map/ppermute | solution.py:42
  77.1 85.0 %collective-permute-start.6 = (bf16[15,256,256]{2,1,0:T(8,128)(2,1)S(1)}, bf16[15,256,256]{2,1,0:T(8,128)(2,1)S(1)}, u32[]{:S(2)}, u32[]{:S(2)}) collective-permute-start(bf16[15,256,256]{2,1,0:T(8,128)(2,1)S(1)} %get-tuple-element.15), channel_id=1, source_target_pairs={{4,0},{8,4},{12,8},{16,12},{20,16},{24,20},{28,24},{5,1},{9,5},{13... | collective-permute-start | bytes 5898248 | tf_op jit(solution)/shard_map/ppermute | solution.py:44
  179.6 0.7 copy-start.4
  179.6 46.8 %copy-start = (f32[16,64,256]{2,1,0:T(8,128)S(1)}, f32[16,64,256]{2,1,0:T(8,128)}, u32[]{:S(2)}) copy-start(f32[16,64,256]{2,1,0:T(8,128)} %param.7) | copy-start | bytes 3145732
Sparse Core Ops, SparseCore 0:
  179.8 46.6 reduce-scatter.1
